TPU v7x, 32 devices: a whole 2x2x4 slice. The times are simulated.
32 devices in a mesh: blk: 16 (over z, y, core), tp: 2 (over x).
Axes of the slice: x: 2, y: 2, z: 4, core: 2. Of those that a mesh axis runs over, the one named last changes fastest.
Arguments:
- frames: bfloat16 [4096, 1024], P('blk'), may hold values from -6 to 6
- clip_lengths: int32 [8], replicated, may hold values from 1 to 3841, 4096 in all
- text_states: bfloat16 [128, 1024], replicated, may hold values from -6 to 6
- text_segments: int32 [128], replicated, may hold values from 0 to 7, never falling along the last dimension, each value on 1 to 32 neighbouring positions
- gain_one: float32 [1024], replicated, may hold values from 0.1 to 1.9
- shift_one: float32 [1024], replicated, may hold values from -1.5 to 1.5
- gain_two: float32 [1024], replicated, may hold values from 0.1 to 1.9
- shift_two: float32 [1024], replicated, may hold values from -1.5 to 1.5
- gain_three: float32 [1024], replicated, may hold values from 0.1 to 1.9
- shift_three: float32 [1024], replicated, may hold values from -1.5 to 1.5
- query_weight: bfloat16 [1024, 1024], P(None, 'tp'), may hold values from -0.1875 to 0.1875
- key_weight: bfloat16 [1024, 1024], P(None, 'tp'), may hold values from -0.1875 to 0.1875
- value_weight: bfloat16 [1024, 1024], P(None, 'tp'), may hold values from -0.1875 to 0.1875
- output_weight: bfloat16 [1024, 1024], P('tp'), may hold values from -0.75 to 0.75
- cross_query: bfloat16 [1024, 1024], P(None, 'tp'), may hold values from -0.1875 to 0.1875
- cross_key: bfloat16 [1024, 1024], P(None, 'tp'), may hold values from -0.1875 to 0.1875
- cross_value: bfloat16 [1024, 1024], P(None, 'tp'), may hold values from -0.1875 to 0.1875
- cross_output: bfloat16 [1024, 1024], P('tp'), may hold values from -0.375 to 0.375
- inner_weight: bfloat16 [1024, 4096], P(None, 'tp'), may hold values from -0.1875 to 0.1875
- outer_weight: bfloat16 [4096, 1024], P('tp'), may hold values from -0.09375 to 0.09375
- cotangent: bfloat16 [4096, 1024], P('blk'), may hold values from -6 to 6
Outputs:
- result: bfloat16 [4096, 1024], P('blk')
- grad_frames: bfloat16 [4096, 1024], P('blk')
- grad_text: float32 [128, 1024], replicated
- grad_gain_one: float32 [1024], replicated
- grad_shift_one: float32 [1024], replicated
- grad_gain_two: float32 [1024], replicated
- grad_shift_two: float32 [1024], replicated
- grad_gain_three: float32 [1024], replicated
- grad_shift_three: float32 [1024], replicated
- grad_query_weight: float32 [1024, 1024], P(None, 'tp')
- grad_key_weight: float32 [1024, 1024], P(None, 'tp')
- grad_value_weight: float32 [1024, 1024], P(None, 'tp')
- grad_output_weight: float32 [1024, 1024], P('tp')
- grad_cross_query: float32 [1024, 1024], P(None, 'tp')
- grad_cross_key: float32 [1024, 1024], P(None, 'tp')
- grad_cross_value: float32 [1024, 1024], P(None, 'tp')
- grad_cross_output: float32 [1024, 1024], P('tp')
- grad_inner_weight: float32 [1024, 4096], P(None, 'tp')
- grad_outer_weight: float32 [4096, 1024], P('tp')
Inputs may be any that keep to these rules, and one draw needn't show every extreme that they name: `clip_lengths`: clips follow one another in the pack; one of them has 3841 frames. `text_segments`: text tokens of a clip stand together and in clip order; every clip has 1 to 32 of them, one exactly 32.
All inputs are finite; a program needn't handle non-finite values.
Results may differ from a plain program's by a relative error of at most 0.028.
Values may be sent and summed in bfloat16 or wider, within the bound.
No kernel may reach another device: no remote copies, remote signals or barrier semaphores. Data moves between devices by JAX's collectives and lax.ppermute only.
A program may use at most 384 MiB of HBM per device.

v0:
```python
import jax
import jax.numpy as jnp
from jax import lax
from jax.sharding import PartitionSpec as P

HEAD_DIM = 64
EPSILON = 1e-05
NEGATIVE = -1e30


def shifted(block, axis, distance):
    devices = range(lax.axis_size(axis))
    route = [(i - distance, i) for i in devices if i - distance in devices]
    return lax.ppermute(block, axis, route)


def shifted_2(value, axis, by):
    size = lax.axis_size(axis)
    return lax.ppermute(value, axis, [(i, (i + by) % size) for i in range(size)])


def layer_norm(values, gain, shift):
    centre = values - jnp.mean(values, axis=-1, keepdims=True)
    spread = jnp.mean(centre * centre, axis=-1, keepdims=True)
    return centre * lax.rsqrt(spread + EPSILON) * gain + shift


def norm_grads(values, gain, shift, grad):
    _, pullback = jax.vjp(layer_norm, values, gain, shift)
    return pullback(grad)


def gelu_exact(values):
    return jax.nn.gelu(values, approximate=False)


def clip_rows(positions, clip_lengths):
    ends = jnp.cumsum(clip_lengths)
    starts = ends - clip_lengths
    segment = jnp.sum((positions[:, None] >= ends[None, :]).astype(jnp.int32), axis=1)
    match = segment[:, None] == jnp.arange(clip_lengths.shape[0], dtype=jnp.int32)[None, :]
    first = jnp.sum(jnp.where(match, starts[None, :], 0), axis=1)
    return (segment, first)


def matmul(left, right):
    return jnp.dot(left, right, preferred_element_type=jnp.float32)


def head_sum(values):
    return lax.psum(values.astype(jnp.bfloat16), "tp").astype(jnp.float32)


def unchanged(state):
    return state


def block_grads(
    query_heads,
    grad_heads,
    log_total,
    delta,
    query_rows,
    query_first,
    key_heads,
    value_heads,
    key_rows,
):
    allowed = (key_rows[None, :] <= query_rows[:, None]) & (
        key_rows[None, :] >= query_first[:, None]
    )
    score = jnp.einsum("qhd,khd->hqk", query_heads, key_heads, preferred_element_type=jnp.float32)
    weights = jnp.exp(jnp.where(allowed[None], score - log_total[:, :, None], NEGATIVE))
    grad_weights = jnp.einsum(
        "qhd,khd->hqk", grad_heads, value_heads, preferred_element_type=jnp.float32
    )
    grad_score = (weights * (grad_weights - delta[:, :, None])).astype(jnp.bfloat16)
    query_part = jnp.einsum(
        "hqk,khd->qhd", grad_score, key_heads, preferred_element_type=jnp.float32
    )
    key_part = jnp.einsum(
        "hqk,qhd->khd", grad_score, query_heads, preferred_element_type=jnp.float32
    )
    value_part = jnp.einsum(
        "hqk,qhd->khd", weights.astype(jnp.bfloat16), grad_heads, preferred_element_type=jnp.float32
    )
    return (query_part, key_part, value_part)


def shards(
    frames,
    clip_lengths,
    text_states,
    text_segments,
    gain_one,
    shift_one,
    gain_two,
    shift_two,
    gain_three,
    shift_three,
    query_weight,
    key_weight,
    value_weight,
    output_weight,
    cross_query,
    cross_key,
    cross_value,
    cross_output,
    inner_weight,
    outer_weight,
    cotangent,
):
    row_count = frames.shape[0]
    text_count = text_states.shape[0]
    width_here = query_weight.shape[1]
    heads_here = width_here // HEAD_DIM
    blk_count = lax.axis_size("blk")
    blk_index = lax.axis_index("blk")
    scale = float(HEAD_DIM) ** (-0.5)
    my_first_row = blk_index * row_count
    offsets = jnp.arange(row_count, dtype=jnp.int32)
    rows = my_first_row + offsets
    segment, first = clip_rows(rows, clip_lengths)
    inputs = frames.astype(jnp.float32)
    normed_one = layer_norm(inputs, gain_one, shift_one).astype(jnp.bfloat16)
    queries = (matmul(normed_one, query_weight) * scale).astype(jnp.bfloat16)
    keys = matmul(normed_one, key_weight).astype(jnp.bfloat16)
    values = matmul(normed_one, value_weight).astype(jnp.bfloat16)
    query_heads = queries.reshape(row_count, heads_here, HEAD_DIM)
    start_state = (
        jnp.zeros((row_count, heads_here, HEAD_DIM), jnp.float32),
        jnp.full((heads_here, row_count), NEGATIVE, jnp.float32),
        jnp.zeros((heads_here, row_count), jnp.float32),
    )
    start = jnp.int32(0)
    key_piece = lax.all_gather(keys, "blk", axis=0, tiled=True)
    value_piece = lax.all_gather(values, "blk", axis=0, tiled=True)
    count = key_piece.shape[0]
    key_rows = jnp.arange(count, dtype=jnp.int32)

    def fold_work(state):
        totals, run_max, run_sum = state
        piece_keys = key_piece.reshape(count, heads_here, HEAD_DIM)
        piece_values = value_piece.reshape(count, heads_here, HEAD_DIM)
        score = jnp.einsum(
            "qhd,khd->hqk", query_heads, piece_keys, preferred_element_type=jnp.float32
        )
        allowed = (key_rows[None, :] <= rows[:, None]) & (key_rows[None, :] >= first[:, None])
        masked = jnp.where(allowed[None], score, NEGATIVE)
        new_max = jnp.maximum(run_max, jnp.max(masked, axis=-1))
        expo = jnp.where(allowed[None], jnp.exp(masked - new_max[:, :, None]), 0.0)
        run_sum = jnp.sum(expo, axis=-1)
        added = jnp.einsum(
            "hqk,khd->qhd",
            expo.astype(jnp.bfloat16),
            piece_values,
            preferred_element_type=jnp.float32,
        )
        totals = added
        return (totals, new_max, run_sum)

    needed = (start <= rows[-1]) & (start + count - 1 >= first[0])
    totals, run_max, run_sum = lax.cond(needed, fold_work, unchanged, start_state)
    self_out = totals / jnp.transpose(run_sum)[:, :, None]
    log_total = run_max + jnp.log(run_sum)
    attended = self_out.reshape(row_count, width_here).astype(jnp.bfloat16)
    first_sum = inputs + head_sum(matmul(attended, output_weight))
    normed_two = layer_norm(first_sum, gain_two, shift_two).astype(jnp.bfloat16)
    cross_queries = (matmul(normed_two, cross_query) * scale).astype(jnp.bfloat16)
    text_keys = matmul(text_states, cross_key).astype(jnp.bfloat16)
    text_values = matmul(text_states, cross_value).astype(jnp.bfloat16)
    cross_heads = cross_queries.reshape(row_count, heads_here, HEAD_DIM)
    text_key_heads = text_keys.reshape(text_count, heads_here, HEAD_DIM)
    text_value_heads = text_values.reshape(text_count, heads_here, HEAD_DIM)
    allowed_text = segment[:, None] == text_segments[None, :]
    cross_score = jnp.einsum(
        "qhd,khd->hqk", cross_heads, text_key_heads, preferred_element_type=jnp.float32
    )
    cross_masked = jnp.where(allowed_text[None], cross_score, NEGATIVE)
    cross_max = jnp.max(cross_masked, axis=-1, keepdims=True)
    cross_expo = jnp.where(allowed_text[None], jnp.exp(cross_masked - cross_max), 0.0)
    cross_weights = cross_expo / jnp.sum(cross_expo, axis=-1, keepdims=True)
    cross_weights_low = cross_weights.astype(jnp.bfloat16)
    cross_out = jnp.einsum(
        "hqk,khd->qhd", cross_weights_low, text_value_heads, preferred_element_type=jnp.float32
    )
    crossed = cross_out.reshape(row_count, width_here).astype(jnp.bfloat16)
    second_sum = first_sum + head_sum(matmul(crossed, cross_output))
    normed_three = layer_norm(second_sum, gain_three, shift_three).astype(jnp.bfloat16)
    hidden_pre = matmul(normed_three, inner_weight)
    hidden = gelu_exact(hidden_pre).astype(jnp.bfloat16)
    output = second_sum + head_sum(matmul(hidden, outer_weight))
    grad_output = cotangent.astype(jnp.float32)
    grad_outer = matmul(hidden.T, cotangent)
    grad_hidden = matmul(cotangent, outer_weight.T)
    _, gelu_back = jax.vjp(gelu_exact, hidden_pre)
    grad_pre = gelu_back(grad_hidden)[0].astype(jnp.bfloat16)
    grad_inner = matmul(normed_three.T, grad_pre)
    grad_normed_three = head_sum(matmul(grad_pre, inner_weight.T))
    through_three, grad_gain_three, grad_shift_three = norm_grads(
        second_sum, gain_three, shift_three, grad_normed_three
    )
    grad_second = grad_output + through_three
    grad_second_low = grad_second.astype(jnp.bfloat16)
    grad_cross_output = matmul(crossed.T, grad_second_low)
    grad_crossed = (
        matmul(grad_second_low, cross_output.T)
        .astype(jnp.bfloat16)
        .reshape(row_count, heads_here, HEAD_DIM)
    )
    grad_cross_weights = jnp.einsum(
        "qhd,khd->hqk", grad_crossed, text_value_heads, preferred_element_type=jnp.float32
    )
    cross_delta = jnp.transpose(jnp.sum(grad_crossed.astype(jnp.float32) * cross_out, axis=-1))
    grad_cross_score = (cross_weights * (grad_cross_weights - cross_delta[:, :, None])).astype(
        jnp.bfloat16
    )
    grad_cross_heads = jnp.einsum(
        "hqk,khd->qhd", grad_cross_score, text_key_heads, preferred_element_type=jnp.float32
    ).astype(jnp.bfloat16)
    grad_cross_queries = (grad_cross_heads * scale).reshape(row_count, width_here)
    text_key_part = jnp.einsum(
        "hqk,qhd->khd", grad_cross_score, cross_heads, preferred_element_type=jnp.float32
    )
    text_value_part = jnp.einsum(
        "hqk,qhd->khd", cross_weights_low, grad_crossed, preferred_element_type=jnp.float32
    )
    grad_text_keys, grad_text_values = lax.psum(
        (
            text_key_part.reshape(text_count, width_here),
            text_value_part.reshape(text_count, width_here),
        ),
        "blk",
    )
    grad_text_keys = grad_text_keys.astype(jnp.bfloat16)
    grad_text_values = grad_text_values.astype(jnp.bfloat16)
    grad_cross_key = matmul(text_states.T, grad_text_keys)
    grad_cross_value = matmul(text_states.T, grad_text_values)
    grad_text = lax.psum(
        (matmul(grad_text_keys, cross_key.T) + matmul(grad_text_values, cross_value.T)).astype(
            jnp.bfloat16
        ),
        "tp",
    ).astype(jnp.float32)
    grad_cross_query = matmul(normed_two.T, grad_cross_queries)
    grad_normed_two = head_sum(matmul(grad_cross_queries, cross_query.T))
    through_two, grad_gain_two, grad_shift_two = norm_grads(
        first_sum, gain_two, shift_two, grad_normed_two
    )
    grad_first = grad_second + through_two
    grad_first_low = grad_first.astype(jnp.bfloat16)
    grad_output_weight = matmul(attended.T, grad_first_low)
    grad_attended = matmul(grad_first_low, output_weight.T).astype(jnp.bfloat16)
    grad_heads = grad_attended.reshape(row_count, heads_here, HEAD_DIM)
    self_delta = jnp.transpose(jnp.sum(grad_heads.astype(jnp.float32) * self_out, axis=-1))
    zero_block = jnp.zeros((row_count, width_here), jnp.float32)

    def key_turn(turn, carry):
        source = (blk_index - turn) % blk_count
        base = source * row_count

        def key_work(state):
            key_block, value_block, key_grad, value_grad, query_grad = state
            query_part, key_part, value_part = block_grads(
                query_heads,
                grad_heads,
                log_total,
                self_delta,
                rows,
                first,
                key_block.reshape(row_count, heads_here, HEAD_DIM),
                value_block.reshape(row_count, heads_here, HEAD_DIM),
                base + offsets,
            )
            return (
                key_block,
                value_block,
                key_grad + key_part.reshape(row_count, width_here),
                value_grad + value_part.reshape(row_count, width_here),
                query_grad + query_part.reshape(row_count, width_here),
            )

        needed = (base <= rows[-1]) & (base + row_count - 1 >= first[0])
        key_block, value_block, key_grad, value_grad, query_grad = lax.cond(
            needed, key_work, unchanged, carry
        )
        key_block, value_block = shifted((key_block, value_block), "blk", 1)
        key_grad, value_grad = (
            shifted_2(key_grad.astype(jnp.bfloat16), "blk", 1).astype(key_grad.dtype),
            shifted_2(value_grad.astype(jnp.bfloat16), "blk", 1).astype(value_grad.dtype),
        )
        return (key_block, value_block, key_grad, value_grad, query_grad)

    final = lax.fori_loop(
        0, blk_count, key_turn, (keys, values, zero_block, zero_block, zero_block)
    )
    key_total, value_total, query_total = (final[2], final[3], final[4])
    grad_queries = query_total.astype(jnp.bfloat16) * scale
    grad_keys = key_total.astype(jnp.bfloat16)
    grad_values = value_total.astype(jnp.bfloat16)
    grad_query_weight = matmul(normed_one.T, grad_queries)
    grad_key_weight = matmul(normed_one.T, grad_keys)
    grad_value_weight = matmul(normed_one.T, grad_values)
    grad_normed_one = head_sum(
        matmul(grad_queries, query_weight.T)
        + matmul(grad_keys, key_weight.T)
        + matmul(grad_values, value_weight.T)
    )
    through_one, grad_gain_one, grad_shift_one = norm_grads(
        inputs, gain_one, shift_one, grad_normed_one
    )
    grad_frames = (grad_first + through_one).astype(jnp.bfloat16)
    (
        grad_query_weight,
        grad_key_weight,
        grad_value_weight,
        grad_output_weight,
        grad_cross_query,
        grad_cross_output,
        grad_inner,
        grad_outer,
        grad_gain_one,
        grad_shift_one,
        grad_gain_two,
        grad_shift_two,
        grad_gain_three,
        grad_shift_three,
    ) = lax.psum(
        (
            grad_query_weight,
            grad_key_weight,
            grad_value_weight,
            grad_output_weight,
            grad_cross_query,
            grad_cross_output,
            grad_inner,
            grad_outer,
            grad_gain_one,
            grad_shift_one,
            grad_gain_two,
            grad_shift_two,
            grad_gain_three,
            grad_shift_three,
        ),
        "blk",
    )
    return (
        output.astype(jnp.bfloat16),
        grad_frames,
        grad_text,
        grad_gain_one,
        grad_shift_one,
        grad_gain_two,
        grad_shift_two,
        grad_gain_three,
        grad_shift_three,
        grad_query_weight,
        grad_key_weight,
        grad_value_weight,
        grad_output_weight,
        grad_cross_query,
        grad_cross_key,
        grad_cross_value,
        grad_cross_output,
        grad_inner,
        grad_outer,
    )


def solution(mesh):
    return jax.shard_map(
        shards,
        mesh=mesh,
        in_specs=(
            P("blk", None),
            P(),
            P(),
            P(),
            P(),
            P(),
            P(),
            P(),
            P(),
            P(),
            P(None, "tp"),
            P(None, "tp"),
            P(None, "tp"),
            P("tp", None),
            P(None, "tp"),
            P(None, "tp"),
            P(None, "tp"),
            P("tp", None),
            P(None, "tp"),
            P("tp", None),
            P("blk", None),
        ),
        out_specs=(
            P("blk", None),
            P("blk", None),
            P(),
            P(),
            P(),
            P(),
            P(),
            P(),
            P(),
            P(None, "tp"),
            P(None, "tp"),
            P(None, "tp"),
            P("tp", None),
            P(None, "tp"),
            P(None, "tp"),
            P(None, "tp"),
            P("tp", None),
            P(None, "tp"),
            P("tp", None),
        ),
        check_vma=False,
    )
```

profile of v0, /device:TPU:0, one launch (start us, length us, event | category | flops | bytes accessed | tf_op | source)
XLA Modules:
  0.0 1468.9 jit_solution(12834105977165518617)
XLA Ops:
  21.8 44.2 %all-gather.3.cloned.1.call-done = bf16[4096,512]{1,0:T(8,128)(2,1)} async-done(((bf16[256,512]{1,0:T(8,128)(2,1)}), bf16[4096,512]{1,0:T(8,128)(2,1)}) %all-gather.3.cloned.1.call-update) | async-done | bytes 4194320 | tf_op jit(solution)/shard_map/all_gather | solution.py:136
  66.1 51.8 %all-gather.5.cloned.1.call-done = bf16[4096,512]{1,0:T(8,128)(2,1)} async-done(((bf16[256,512]{1,0:T(8,128)(2,1)}), bf16[4096,512]{1,0:T(8,128)(2,1)}) %all-gather.5.cloned.1.call-update) | async-done | bytes 4194320 | tf_op jit(solution)/shard_map/all_gather | solution.py:137
  117.9 62.9 %conditional.2 = (f32[256,8,64]{0,2,1:T(8,128)S(1)}, f32[8,256]{1,0:T(8,128)}, f32[8,256]{1,0:T(8,128)}, f32[8,256]{1,0:T(8,128)S(1)}) conditional(s32[]{:T(128)} %bitcast.13, () %tuple.55, (s32[4096]{0:T(1024)S(1)}, s32[4096]{0:T(1024)S(1)}, s32[256]{0:T(256)}, s32[256]{0:T(256)}, bf16[4096,512]{1,0:T(8,128)(2,1)}, ...), branch_computations={%region_5.6_spmd, %region_6.9_spmd} | conditional | flops 2234513408 | bytes 130910240 | solution.py:163
  117.9 6.3 copy.81
  125.8 6.3 copy.80
  132.2 15.7 %select_reduce_fusion = (f32[8,256]{1,0:T(8,128)S(1)}, f32[8,256,4096]{2,1,0:T(8,128)}) fusion(pred[256,4096]{1,0:T(8,128)(4,1)S(1)} %compare_and_fusion, bf16[256,8,64]{0,2,1:T(8,128)(2,1)S(1)} %get-tuple-element.475, bf16[4096,8,64]{0,2,1:T(8,128)(2,1)} %bitcast.126), kind=kOutput, calls=%fused_computation.2 | convolution fusion | flops 1090516992 | bytes 39067648 | tf_op jit(solution)/shard_map/cond/branch_1_fun/qhd,khd->hqk/dot_general | solution.py:145
  148.4 15.5 %fusion.7 = f32[256,8,64]{0,2,1:T(8,128)S(1)} fusion(bf16[4096,8,64]{0,2,1:T(8,128)(2,1)} %bitcast.133, f32[8,256,4096]{2,1,0:T(8,128)} %get-tuple-element.768, f32[8,256]{1,0:T(8,128)} %broadcast_maximum_fusion, pred[256,4096]{1,0:T(8,128)(4,1)S(1)} %compare_and_fusion), kind=kOutput, calls=%fused_computation.8 | convolution fusion | flops 1107296256 | bytes 39329792 | tf_op jit(solution)/shard_map/cond/branch_1_fun/hqk,khd->qhd/dot_general | solution.py:153
  163.9 16.2 %fusion.2 = f32[8,256]{1,0:T(8,128)} fusion(f32[8,256,4096]{2,1,0:T(8,128)} %get-tuple-element.768, f32[8,256]{1,0:T(8,128)} %broadcast_maximum_fusion, pred[256,4096]{1,0:T(8,128)(4,1)S(1)} %compare_and_fusion), kind=kLoop, calls=%fused_computation.3 | loop fusion | flops 33552384 | bytes 34619392 | tf_op jit(solution)/shard_map/cond/branch_1_fun/reduce_sum | solution.py:152
  189.6 21.9 %all-reduce.12.cloned.1.call-done = bf16[256,1024]{1,0:T(8,128)(2,1)} async-done(((bf16[256,1024]{1,0:T(8,128)(2,1)}), bf16[256,1024]{1,0:T(8,128)(2,1)}) %all-reduce.12.cloned.1.call-update) | async-done | bytes 524304 | tf_op jit(solution)/shard_map/psum | solution.py:51
  228.4 25.3 %all-reduce.14.cloned.1.call-done = bf16[256,1024]{1,0:T(8,128)(2,1)} async-done(((bf16[256,1024]{1,0:T(8,128)(2,1)}), bf16[256,1024]{1,0:T(8,128)(2,1)}) %all-reduce.14.cloned.1.call-update) | async-done | bytes 524304 | tf_op jit(solution)/shard_map/psum | solution.py:51
  256.5 3.7 fusion.86
  260.2 6.6 add_convert_fusion
  271.9 6.2 fusion.105
  280.3 4.8 fusion.85
  285.1 15.5 %all-reduce.16.cloned.1.call-done = bf16[256,1024]{1,0:T(8,128)(2,1)} async-done(((bf16[256,1024]{1,0:T(8,128)(2,1)}), bf16[256,1024]{1,0:T(8,128)(2,1)}) %all-reduce.16.cloned.1.call-update) | async-done | bytes 524304 | tf_op jit(solution)/shard_map/psum | solution.py:51
  317.8 25.6 %all-reduce.18.cloned.1.call-done = bf16[256,1024]{1,0:T(8,128)(2,1)} async-done(((bf16[256,1024]{1,0:T(8,128)(2,1)}), bf16[256,1024]{1,0:T(8,128)(2,1)}) %all-reduce.18.cloned.1.call-update) | async-done | bytes 524304 | tf_op jit(solution)/shard_map/psum | solution.py:51
  353.3 421.7 %while.26 = (s32[]{:T(128)}, bf16[256,512]{0,1:T(8,128)(2,1)S(1)}, bf16[256,512]{0,1:T(8,128)(2,1)}, f32[256,512]{0,1:T(8,128)}, f32[256,512]{0,1:T(8,128)}, /*i...) while((s32[]{:T(128)}, bf16[256,512]{0,1:T(8,128)(2,1)S(1)}, ...), condition=%wide.region_29.30_spmd.clone, body=%wide.region_26.29_spmd.clone.sunk | while | flops 341115168 | bytes 37714808 | solution.py:294
  359.2 5.0 conditional.5
  368.5 3.5 collective-permute-start.1
  384.2 6.3 collective-permute-start.2
  395.5 4.4 collective-permute-start.1
  413.3 7.3 collective-permute-start.3
  422.6 5.2 collective-permute-start.1
  443.0 7.5 collective-permute-start
  450.5 5.2 collective-permute-start.1
  473.5 10.1 collective-permute-start.1
  501.4 5.2 collective-permute-start.1
  525.6 5.2 collective-permute-start.1
  543.6 6.3 collective-permute-start.3
  549.9 3.6 collective-permute-start
  553.5 5.2 collective-permute-start.1
  573.9 7.4 collective-permute-start
  581.3 5.2 collective-permute-start.1
  604.4 9.1 collective-permute-start.1
  632.3 5.2 collective-permute-start.1
  656.4 5.2 collective-permute-start.1
  674.5 5.3 collective-permute-start.3
  679.7 4.6 collective-permute-start
  684.3 5.2 collective-permute-start.1
  704.7 7.4 collective-permute-start
  712.2 5.2 collective-permute-start.1
  735.2 8.1 collective-permute-start.1
  763.1 5.2 collective-permute-start.1
  784.6 31.8 %all-reduce.20.cloned.1.call-done = bf16[256,1024]{1,0:T(8,128)(2,1)} async-done(((bf16[256,1024]{1,0:T(8,128)(2,1)}), bf16[256,1024]{1,0:T(8,128)(2,1)}) %all-reduce.20.cloned.1.call-update) | async-done | bytes 524304 | tf_op jit(solution)/shard_map/psum | solution.py:51
  820.2 67.9 %all-reduce.25 = (bf16[128,512]{0,1:T(8,128)(2,1)S(1)}, bf16[128,512]{0,1:T(8,128)(2,1)}, f32[1024]{0:T(1024)}, f32[1024]{0:T(1024)}, f32[1024]{0:T(1024)}, /*in...) all-reduce(f32[128,512]{0,1:T(8,128)S(1)} %bitcast.142, ...), channel_id=1, replica_groups=mesh['blk'=16,'tp'=2] {'blk'}, use_global_device_ids=true, to_apply=%region_33.34 | all-reduce | flops 137216 | bytes 835584 | tf_op jit(solution)/shard_map/psum | solution.py:228
  909.3 13.6 all-reduce.24.cloned.1.call-done
  926.7 512.8 %all-reduce.22.cloned.1.call-done = (f32[1024,512]{1,0:T(8,128)}, f32[1024,512]{1,0:T(8,128)}, f32[1024,512]{1,0:T(8,128)}, f32[512,1024]{1,0:T(8,128)}, f32[102...) async-done(((f32[1024,512]{1,0:T(8,128)}, f32[1024,512]{1,0:T(8,128)}, f32[1024,512]{1,0:T(8,128)}, f32[512,1024]{1,0:T(8,128)}, ...) | async-done | bytes 29360144 | tf_op jit(solution)/shard_map/psum | solution.py:328
  1453.1 4.3 copy.164
  (696 shorter events, 385.8 us)
Async XLA Ops:
  7.3 58.8 %all-gather.3.cloned.1.call-start = ((), (), s32[]{:S(2)}) async-start(), calls=%async_computation | async-start | bytes 4456448 | tf_op jit(solution)/shard_map/all_gather | solution.py:136
  12.7 105.2 %all-gather.5.cloned.1.call-start = ((), (), s32[]{:S(2)}) async-start(), calls=%async_computation.1 | async-start | bytes 4456448 | tf_op jit(solution)/shard_map/all_gather | solution.py:137
  14.0 197.5 %all-reduce.12.cloned.1.call-start = ((), (), s32[]{:S(2)}) async-start(), calls=%async_computation.2 | async-start | bytes 1048576 | tf_op jit(solution)/shard_map/psum | solution.py:51
  184.3 69.4 %all-reduce.14.cloned.1.call-start = ((), (), s32[]{:S(2)}) async-start(), calls=%async_computation.3 | async-start | bytes 1048576 | tf_op jit(solution)/shard_map/psum | solution.py:51
  224.9 75.7 %all-reduce.16.cloned.1.call-start = ((), (), s32[]{:S(2)}) async-start(), calls=%async_computation.4 | async-start | bytes 1048576 | tf_op jit(solution)/shard_map/psum | solution.py:51
  271.9 71.5 %all-reduce.18.cloned.1.call-start = ((), (), s32[]{:S(2)}) async-start(), calls=%async_computation.5 | async-start | bytes 1048576 | tf_op jit(solution)/shard_map/psum | solution.py:51
  314.6 501.9 %all-reduce.20.cloned.1.call-start = ((), (), s32[]{:S(2)}) async-start(), calls=%async_computation.6 | async-start | bytes 1048576 | tf_op jit(solution)/shard_map/psum | solution.py:51
  384.2 15.7 %collective-permute-start.2 = (bf16[256,512]{0,1:T(8,128)(2,1)S(1)}, bf16[256,512]{0,1:T(8,128)(2,1)}, u32[]{:S(2)}, u32[]{:S(2)}) collective-permute-start(bf16[256,512]{0,1:T(8,128)(2,1)S(1)} %convert_element_type.500), channel_id=1, source_target_pairs={{0,2},{2,4},{4,6},{6,8},{8,10},{10,12},{12,14},{14,16},{16,18},{18... | collective-permute-start | bytes 786440 | tf_op jit(solution)/shard_map/while/body/eval_jaxpr/ppermute | solution.py:19
  410.3 17.5 %collective-permute-start.2 = (bf16[256,512]{0,1:T(8,128)(2,1)S(1)}, bf16[256,512]{0,1:T(8,128)(2,1)}, u32[]{:S(2)}, u32[]{:S(2)}) collective-permute-start(bf16[256,512]{0,1:T(8,128)(2,1)S(1)} %convert_element_type.500), channel_id=1, source_target_pairs={{0,2},{2,4},{4,6},{6,8},{8,10},{10,12},{12,14},{14,16},{16,18},{18... | collective-permute-start | bytes 786440 | tf_op jit(solution)/shard_map/while/body/eval_jaxpr/ppermute | solution.py:19
  413.3 16.3 %collective-permute-start.3 = (bf16[256,512]{0,1:T(8,128)(2,1)}, bf16[256,512]{0,1:T(8,128)(2,1)S(1)}, u32[]{:S(2)}, u32[]{:S(2)}) collective-permute-start(bf16[256,512]{0,1:T(8,128)(2,1)} %convert_element_type.502), channel_id=1, source_target_pairs={{0,2},{2,4},{4,6},{6,8},{8,10},{10,12},{12,14},{14,16},{16,18},{18... | collective-permute-start | bytes 786440 | tf_op jit(solution)/shard_map/while/body/eval_jaxpr/ppermute | solution.py:19
  438.2 17.5 %collective-permute-start.2 = (bf16[256,512]{0,1:T(8,128)(2,1)S(1)}, bf16[256,512]{0,1:T(8,128)(2,1)}, u32[]{:S(2)}, u32[]{:S(2)}) collective-permute-start(bf16[256,512]{0,1:T(8,128)(2,1)S(1)} %convert_element_type.500), channel_id=1, source_target_pairs={{0,2},{2,4},{4,6},{6,8},{8,10},{10,12},{12,14},{14,16},{16,18},{18... | collective-permute-start | bytes 786440 | tf_op jit(solution)/shard_map/while/body/eval_jaxpr/ppermute | solution.py:19
  440.7 16.8 %collective-permute-start.3 = (bf16[256,512]{0,1:T(8,128)(2,1)}, bf16[256,512]{0,1:T(8,128)(2,1)S(1)}, u32[]{:S(2)}, u32[]{:S(2)}) collective-permute-start(bf16[256,512]{0,1:T(8,128)(2,1)} %convert_element_type.502), channel_id=1, source_target_pairs={{0,2},{2,4},{4,6},{6,8},{8,10},{10,12},{12,14},{14,16},{16,18},{18... | collective-permute-start | bytes 786440 | tf_op jit(solution)/shard_map/while/body/eval_jaxpr/ppermute | solution.py:19
  443.0 15.3 %collective-permute-start = (bf16[256,512]{0,1:T(8,128)(2,1)S(1)}, bf16[256,512]{0,1:T(8,128)(2,1)S(1)}, u32[]{:S(2)}, u32[]{:S(2)}) collective-permute-start(bf16[256,512]{0,1:T(8,128)(2,1)S(1)} %copy.126), channel_id=1, source_target_pairs={{0,2},{2,4},{4,6},{6,8},{8,10},{10,12},{12,14},{14,16},{16,18},{18... | collective-permute-start | bytes 786440 | tf_op jit(solution)/shard_map/while/body/eval_jaxpr/ppermute | solution.py:14
  466.1 17.5 %collective-permute-start.2 = (bf16[256,512]{0,1:T(8,128)(2,1)S(1)}, bf16[256,512]{0,1:T(8,128)(2,1)}, u32[]{:S(2)}, u32[]{:S(2)}) collective-permute-start(bf16[256,512]{0,1:T(8,128)(2,1)S(1)} %convert_element_type.500), channel_id=1, source_target_pairs={{0,2},{2,4},{4,6},{6,8},{8,10},{10,12},{12,14},{14,16},{16,18},{18... | collective-permute-start | bytes 786440 | tf_op jit(solution)/shard_map/while/body/eval_jaxpr/ppermute | solution.py:19
  468.6 16.8 %collective-permute-start.3 = (bf16[256,512]{0,1:T(8,128)(2,1)}, bf16[256,512]{0,1:T(8,128)(2,1)S(1)}, u32[]{:S(2)}, u32[]{:S(2)}) collective-permute-start(bf16[256,512]{0,1:T(8,128)(2,1)} %convert_element_type.502), channel_id=1, source_target_pairs={{0,2},{2,4},{4,6},{6,8},{8,10},{10,12},{12,14},{14,16},{16,18},{18... | collective-permute-start | bytes 786440 | tf_op jit(solution)/shard_map/while/body/eval_jaxpr/ppermute | solution.py:19
  470.9 15.3 %collective-permute-start = (bf16[256,512]{0,1:T(8,128)(2,1)S(1)}, bf16[256,512]{0,1:T(8,128)(2,1)S(1)}, u32[]{:S(2)}, u32[]{:S(2)}) collective-permute-start(bf16[256,512]{0,1:T(8,128)(2,1)S(1)} %copy.126), channel_id=1, source_target_pairs={{0,2},{2,4},{4,6},{6,8},{8,10},{10,12},{12,14},{14,16},{16,18},{18... | collective-permute-start | bytes 786440 | tf_op jit(solution)/shard_map/while/body/eval_jaxpr/ppermute | solution.py:14
  473.5 12.7 collective-permute-start.1
  494.0 12.5 collective-permute-start.2
  496.5 11.9 collective-permute-start.3
  517.0 13.8 collective-permute-start.2
  520.6 11.9 collective-permute-start.3
  541.2 17.5 %collective-permute-start.2 = (bf16[256,512]{0,1:T(8,128)(2,1)S(1)}, bf16[256,512]{0,1:T(8,128)(2,1)}, u32[]{:S(2)}, u32[]{:S(2)}) collective-permute-start(bf16[256,512]{0,1:T(8,128)(2,1)S(1)} %convert_element_type.500), channel_id=1, source_target_pairs={{0,2},{2,4},{4,6},{6,8},{8,10},{10,12},{12,14},{14,16},{16,18},{18... | collective-permute-start | bytes 786440 | tf_op jit(solution)/shard_map/while/body/eval_jaxpr/ppermute | solution.py:19
  543.6 16.8 %collective-permute-start.3 = (bf16[256,512]{0,1:T(8,128)(2,1)}, bf16[256,512]{0,1:T(8,128)(2,1)S(1)}, u32[]{:S(2)}, u32[]{:S(2)}) collective-permute-start(bf16[256,512]{0,1:T(8,128)(2,1)} %convert_element_type.502), channel_id=1, source_target_pairs={{0,2},{2,4},{4,6},{6,8},{8,10},{10,12},{12,14},{14,16},{16,18},{18... | collective-permute-start | bytes 786440 | tf_op jit(solution)/shard_map/while/body/eval_jaxpr/ppermute | solution.py:19
  569.1 17.4 %collective-permute-start.2 = (bf16[256,512]{0,1:T(8,128)(2,1)S(1)}, bf16[256,512]{0,1:T(8,128)(2,1)}, u32[]{:S(2)}, u32[]{:S(2)}) collective-permute-start(bf16[256,512]{0,1:T(8,128)(2,1)S(1)} %convert_element_type.500), channel_id=1, source_target_pairs={{0,2},{2,4},{4,6},{6,8},{8,10},{10,12},{12,14},{14,16},{16,18},{18... | collective-permute-start | bytes 786440 | tf_op jit(solution)/shard_map/while/body/eval_jaxpr/ppermute | solution.py:19
  571.5 16.8 %collective-permute-start.3 = (bf16[256,512]{0,1:T(8,128)(2,1)}, bf16[256,512]{0,1:T(8,128)(2,1)S(1)}, u32[]{:S(2)}, u32[]{:S(2)}) collective-permute-start(bf16[256,512]{0,1:T(8,128)(2,1)} %convert_element_type.502), channel_id=1, source_target_pairs={{0,2},{2,4},{4,6},{6,8},{8,10},{10,12},{12,14},{14,16},{16,18},{18... | collective-permute-start | bytes 786440 | tf_op jit(solution)/shard_map/while/body/eval_jaxpr/ppermute | solution.py:19
  573.9 15.2 %collective-permute-start = (bf16[256,512]{0,1:T(8,128)(2,1)S(1)}, bf16[256,512]{0,1:T(8,128)(2,1)S(1)}, u32[]{:S(2)}, u32[]{:S(2)}) collective-permute-start(bf16[256,512]{0,1:T(8,128)(2,1)S(1)} %copy.126), channel_id=1, source_target_pairs={{0,2},{2,4},{4,6},{6,8},{8,10},{10,12},{12,14},{14,16},{16,18},{18... | collective-permute-start | bytes 786440 | tf_op jit(solution)/shard_map/while/body/eval_jaxpr/ppermute | solution.py:14
  597.0 16.5 %collective-permute-start.2 = (bf16[256,512]{0,1:T(8,128)(2,1)S(1)}, bf16[256,512]{0,1:T(8,128)(2,1)}, u32[]{:S(2)}, u32[]{:S(2)}) collective-permute-start(bf16[256,512]{0,1:T(8,128)(2,1)S(1)} %convert_element_type.500), channel_id=1, source_target_pairs={{0,2},{2,4},{4,6},{6,8},{8,10},{10,12},{12,14},{14,16},{16,18},{18... | collective-permute-start | bytes 786440 | tf_op jit(solution)/shard_map/while/body/eval_jaxpr/ppermute | solution.py:19
  599.4 15.9 %collective-permute-start.3 = (bf16[256,512]{0,1:T(8,128)(2,1)}, bf16[256,512]{0,1:T(8,128)(2,1)S(1)}, u32[]{:S(2)}, u32[]{:S(2)}) collective-permute-start(bf16[256,512]{0,1:T(8,128)(2,1)} %convert_element_type.502), channel_id=1, source_target_pairs={{0,2},{2,4},{4,6},{6,8},{8,10},{10,12},{12,14},{14,16},{16,18},{18... | collective-permute-start | bytes 786440 | tf_op jit(solution)/shard_map/while/body/eval_jaxpr/ppermute | solution.py:19
  601.8 14.3 collective-permute-start
  604.4 11.7 collective-permute-start.1
  623.9 13.6 collective-permute-start.2
  627.3 12.0 collective-permute-start.3
  647.9 13.7 collective-permute-start.2
  651.4 12.7 collective-permute-start.3
  672.8 16.7 %collective-permute-start.2 = (bf16[256,512]{0,1:T(8,128)(2,1)S(1)}, bf16[256,512]{0,1:T(8,128)(2,1)}, u32[]{:S(2)}, u32[]{:S(2)}) collective-permute-start(bf16[256,512]{0,1:T(8,128)(2,1)S(1)} %convert_element_type.500), channel_id=1, source_target_pairs={{0,2},{2,4},{4,6},{6,8},{8,10},{10,12},{12,14},{14,16},{16,18},{18... | collective-permute-start | bytes 786440 | tf_op jit(solution)/shard_map/while/body/eval_jaxpr/ppermute | solution.py:19
  674.5 16.8 %collective-permute-start.3 = (bf16[256,512]{0,1:T(8,128)(2,1)}, bf16[256,512]{0,1:T(8,128)(2,1)S(1)}, u32[]{:S(2)}, u32[]{:S(2)}) collective-permute-start(bf16[256,512]{0,1:T(8,128)(2,1)} %convert_element_type.502), channel_id=1, source_target_pairs={{0,2},{2,4},{4,6},{6,8},{8,10},{10,12},{12,14},{14,16},{16,18},{18... | collective-permute-start | bytes 786440 | tf_op jit(solution)/shard_map/while/body/eval_jaxpr/ppermute | solution.py:19
  679.7 12.4 collective-permute-start
  699.9 17.4 %collective-permute-start.2 = (bf16[256,512]{0,1:T(8,128)(2,1)S(1)}, bf16[256,512]{0,1:T(8,128)(2,1)}, u32[]{:S(2)}, u32[]{:S(2)}) collective-permute-start(bf16[256,512]{0,1:T(8,128)(2,1)S(1)} %convert_element_type.500), channel_id=1, source_target_pairs={{0,2},{2,4},{4,6},{6,8},{8,10},{10,12},{12,14},{14,16},{16,18},{18... | collective-permute-start | bytes 786440 | tf_op jit(solution)/shard_map/while/body/eval_jaxpr/ppermute | solution.py:19
  702.4 16.8 %collective-permute-start.3 = (bf16[256,512]{0,1:T(8,128)(2,1)}, bf16[256,512]{0,1:T(8,128)(2,1)S(1)}, u32[]{:S(2)}, u32[]{:S(2)}) collective-permute-start(bf16[256,512]{0,1:T(8,128)(2,1)} %convert_element_type.502), channel_id=1, source_target_pairs={{0,2},{2,4},{4,6},{6,8},{8,10},{10,12},{12,14},{14,16},{16,18},{18... | collective-permute-start | bytes 786440 | tf_op jit(solution)/shard_map/while/body/eval_jaxpr/ppermute | solution.py:19
  704.7 15.2 %collective-permute-start = (bf16[256,512]{0,1:T(8,128)(2,1)S(1)}, bf16[256,512]{0,1:T(8,128)(2,1)S(1)}, u32[]{:S(2)}, u32[]{:S(2)}) collective-permute-start(bf16[256,512]{0,1:T(8,128)(2,1)S(1)} %copy.126), channel_id=1, source_target_pairs={{0,2},{2,4},{4,6},{6,8},{8,10},{10,12},{12,14},{14,16},{16,18},{18... | collective-permute-start | bytes 786440 | tf_op jit(solution)/shard_map/while/body/eval_jaxpr/ppermute | solution.py:14
  727.8 15.5 %collective-permute-start.2 = (bf16[256,512]{0,1:T(8,128)(2,1)S(1)}, bf16[256,512]{0,1:T(8,128)(2,1)}, u32[]{:S(2)}, u32[]{:S(2)}) collective-permute-start(bf16[256,512]{0,1:T(8,128)(2,1)S(1)} %convert_element_type.500), channel_id=1, source_target_pairs={{0,2},{2,4},{4,6},{6,8},{8,10},{10,12},{12,14},{14,16},{16,18},{18... | collective-permute-start | bytes 786440 | tf_op jit(solution)/shard_map/while/body/eval_jaxpr/ppermute | solution.py:19
  730.2 15.3 %collective-permute-start.3 = (bf16[256,512]{0,1:T(8,128)(2,1)}, bf16[256,512]{0,1:T(8,128)(2,1)S(1)}, u32[]{:S(2)}, u32[]{:S(2)}) collective-permute-start(bf16[256,512]{0,1:T(8,128)(2,1)} %convert_element_type.502), channel_id=1, source_target_pairs={{0,2},{2,4},{4,6},{6,8},{8,10},{10,12},{12,14},{14,16},{16,18},{18... | collective-permute-start | bytes 786440 | tf_op jit(solution)/shard_map/while/body/eval_jaxpr/ppermute | solution.py:19
  732.6 13.8 collective-permute-start
  754.2 16.6 %collective-permute-start.2 = (bf16[256,512]{0,1:T(8,128)(2,1)S(1)}, bf16[256,512]{0,1:T(8,128)(2,1)}, u32[]{:S(2)}, u32[]{:S(2)}) collective-permute-start(bf16[256,512]{0,1:T(8,128)(2,1)S(1)} %convert_element_type.500), channel_id=1, source_target_pairs={{0,2},{2,4},{4,6},{6,8},{8,10},{10,12},{12,14},{14,16},{16,18},{18... | collective-permute-start | bytes 786440 | tf_op jit(solution)/shard_map/while/body/eval_jaxpr/ppermute | solution.py:19
  758.1 15.3 %collective-permute-start.3 = (bf16[256,512]{0,1:T(8,128)(2,1)}, bf16[256,512]{0,1:T(8,128)(2,1)S(1)}, u32[]{:S(2)}, u32[]{:S(2)}) collective-permute-start(bf16[256,512]{0,1:T(8,128)(2,1)} %convert_element_type.502), channel_id=1, source_target_pairs={{0,2},{2,4},{4,6},{6,8},{8,10},{10,12},{12,14},{14,16},{16,18},{18... | collective-permute-start | bytes 786440 | tf_op jit(solution)/shard_map/while/body/eval_jaxpr/ppermute | solution.py:19
  760.5 13.8 collective-permute-start
  779.7 143.2 %all-reduce.24.cloned.1.call-start = ((), (), s32[]{:S(2)}) async-start(), calls=%async_computation.8 | async-start | bytes 1572864 | tf_op jit(solution)/shard_map/psum | solution.py:51
  891.9 547.5 %all-reduce.22.cloned.1.call-start = ((), (), s32[]{:S(2)}) async-start(), calls=%async_computation.7 | async-start | bytes 58720256 | tf_op jit(solution)/shard_map/psum | solution.py:328
  (170 other events, 1533.0 us)
Sparse Core Ops, SparseCore 0:
  12.8 53.2 all-gather.2
  68.8 49.0 all-gather.4
  184.4 27.0 all-reduce.11
  225.1 28.5 all-reduce.13
  272.0 28.5 all-reduce.15
  314.7 28.5 all-reduce.17
  779.8 36.5 all-reduce.19
  892.0 30.8 all-reduce.23
  929.9 509.5 all-reduce.21
where the time goes:
time: 1480 us; the launch traced here: 1470 us
  waiting for transfers between devices  749 us (51%)
  starting transfers between devices  234 us (16%)
  local copies, waits for them, and re-layouts  142 us (10%)
  other arithmetic  127 us (9%)
  matrix products  109 us (7%)
  blocking collectives  67.9 us (5%)
  loops' own time  23.5 us (2%)
  between operations  16.3 us (1%)
    psum x1, waiting for transfers between devices, shards(): lax.psum((grad_query_weight, grad_key_weight, grad_value_weight, grad_out...  513 us
    ppermute x32, starting transfers between devices, shifted(): return lax.ppermute(block, axis, route)  149 us
    psum x6, waiting for transfers between devices, head_sum(): return lax.psum(values.astype(jnp.bfloat16), 'tp').astype(jnp.float32)  134 us
    ppermute x32, starting transfers between devices, shifted_2(): lax.ppermute(value, axis, [(i, (i + by) % size) for i in range(size)])  83.7 us
    psum x1, blocking collectives, shards(): lax.psum((text_key_part.reshape(text_count, width_here), text_value_part....  67.9 us
    dot_general x30, matrix products, matmul(): return jnp.dot(left, right, preferred_element_type=jnp.float32)  67 us
    all_gather x1, waiting for transfers between devices, shards(): value_piece = lax.all_gather(values, 'blk', axis=0, tiled=True)  51.8 us
    all_gather x1, waiting for transfers between devices, shards(): key_piece = lax.all_gather(keys, 'blk', axis=0, tiled=True)  44.2 us
  transfers between devices with their start and end apart: 73, of which 15 were waited for; matrix products, arithmetic and copies ran while one was open for 7% of the time, Pallas kernels for 0%

commit v1 on v0

--- a/solution.py
+++ b/solution.py
@@ -48,7 +48,7 @@
 
 
 def head_sum(values):
-    return lax.psum(values.astype(jnp.bfloat16), "tp").astype(jnp.float32)
+    return jnp.sum(lax.all_gather(values.astype(jnp.bfloat16), "tp"), axis=0).astype(jnp.float32)
 
 
 def unchanged(state):

time: 1480 us -> 1410 us (0.953)
  local copies, waits for them, and re-layouts: 142 us -> 115 us
  other arithmetic: 127 us -> 104 us
  waiting for transfers between devices: 749 us -> 728 us
    psum x6 -> x1, waiting for transfers between devices: 134 us -> 6.25 us  [shards(): lax.psum((matmul(grad_text_keys, cross_key.T) + matmul(grad_text_values,...]
    all_gather x0 -> x6, waiting for transfers between devices: none -> 94.6 us  [head_sum(): lax.all_gather(values.astype(jnp.bfloat16), 'tp')]
    while x128 -> x32, local copies, waits for them, and re-layouts: 39.7 us -> 11.6 us
    convert_element_type x16, other arithmetic: 28.5 us -> 0.59 us  [key_turn(): shifted_2(key_grad.astype(jnp.bfloat16), 'blk', 1).astype(key_grad.dtype)]
    convert_element_type x16, other arithmetic: 13.3 us -> 28.4 us  [key_turn(): shifted_2(value_grad.astype(jnp.bfloat16), 'blk', 1)]
    unnamed x198 -> x202, local copies, waits for them, and re-layouts: 39 us -> 43.8 us
  transfers between devices with their start and end apart: 73 -> 74, of which waited for: 15 -> 19; matrix products, arithmetic and copies ran while one was open for 7% -> 7% of each run, Pallas kernels for 0% -> 0%
where the time goes in v1:
time: 1410 us; the launch traced here: 1400 us
  waiting for transfers between devices  728 us (52%)
  starting transfers between devices  236 us (17%)
  local copies, waits for them, and re-layouts  115 us (8%)
  matrix products  107 us (8%)
  other arithmetic  104 us (7%)
  blocking collectives  68.1 us (5%)
  loops' own time  22.6 us (2%)
  between operations  16.8 us (1%)
    psum x1, waiting for transfers between devices, shards(): lax.psum((grad_query_weight, grad_key_weight, grad_value_weight, grad_out...  516 us
    ppermute x32, starting transfers between devices, shifted(): return lax.ppermute(block, axis, route)  152 us
    all_gather x6, waiting for transfers between devices, head_sum(): lax.all_gather(values.astype(jnp.bfloat16), 'tp')  94.6 us
    ppermute x32, starting transfers between devices, shifted_2(): lax.ppermute(value, axis, [(i, (i + by) % size) for i in range(size)])  83 us
    psum x1, blocking collectives, shards(): lax.psum((text_key_part.reshape(text_count, width_here), text_value_part....  68.1 us
    dot_general x30, matrix products, matmul(): return jnp.dot(left, right, preferred_element_type=jnp.float32)  65.8 us
    all_gather x1, waiting for transfers between devices, shards(): value_piece = lax.all_gather(values, 'blk', axis=0, tiled=True)  51.8 us
    all_gather x1, waiting for transfers between devices, shards(): key_piece = lax.all_gather(keys, 'blk', axis=0, tiled=True)  44.2 us
  transfers between devices with their start and end apart: 74, of which 19 were waited for; matrix products, arithmetic and copies ran while one was open for 7% of the time, Pallas kernels for 0%

profile of v1, /device:TPU:0, one launch (start us, length us, event | category | flops | bytes accessed | tf_op | source)
XLA Modules:
  0.0 1398.0 jit_solution(18143351048581168564)
XLA Ops:
  21.8 44.2 %all-gather.15.cloned.1.call-done = bf16[4096,512]{1,0:T(8,128)(2,1)} async-done(((bf16[256,512]{1,0:T(8,128)(2,1)}), bf16[4096,512]{1,0:T(8,128)(2,1)}) %all-gather.15.cloned.1.call-update) | async-done | bytes 4194320 | tf_op jit(solution)/shard_map/all_gather | solution.py:136
  66.1 51.8 %all-gather.17.cloned.1.call-done = bf16[4096,512]{1,0:T(8,128)(2,1)} async-done(((bf16[256,512]{1,0:T(8,128)(2,1)}), bf16[4096,512]{1,0:T(8,128)(2,1)}) %all-gather.17.cloned.1.call-update) | async-done | bytes 4194320 | tf_op jit(solution)/shard_map/all_gather | solution.py:137
  117.9 62.9 %conditional.2 = (f32[256,8,64]{0,2,1:T(8,128)S(1)}, f32[8,256]{1,0:T(8,128)}, f32[8,256]{1,0:T(8,128)}, f32[8,256]{1,0:T(8,128)S(1)}) conditional(s32[]{:T(128)} %bitcast.13, () %tuple.55, (s32[4096]{0:T(1024)S(1)}, s32[4096]{0:T(1024)S(1)}, s32[256]{0:T(256)}, s32[256]{0:T(256)}, bf16[4096,512]{1,0:T(8,128)(2,1)}, ...), branch_computations={%region_5.6_spmd, %region_6.9_spmd} | conditional | flops 2234513408 | bytes 130910240 | solution.py:163
  117.9 6.3 copy.81
  125.8 6.3 copy.80
  132.2 15.6 %select_reduce_fusion = (f32[8,256]{1,0:T(8,128)S(1)}, f32[8,256,4096]{2,1,0:T(8,128)}) fusion(pred[256,4096]{1,0:T(8,128)(4,1)S(1)} %compare_and_fusion, bf16[256,8,64]{0,2,1:T(8,128)(2,1)S(1)} %get-tuple-element.475, bf16[4096,8,64]{0,2,1:T(8,128)(2,1)} %bitcast.132), kind=kOutput, calls=%fused_computation.2 | convolution fusion | flops 1090516992 | bytes 39067648 | tf_op jit(solution)/shard_map/cond/branch_1_fun/qhd,khd->hqk/dot_general | solution.py:145
  148.4 15.5 %fusion.7 = f32[256,8,64]{0,2,1:T(8,128)S(1)} fusion(bf16[4096,8,64]{0,2,1:T(8,128)(2,1)} %bitcast.139, f32[8,256,4096]{2,1,0:T(8,128)} %get-tuple-element.766, f32[8,256]{1,0:T(8,128)} %broadcast_maximum_fusion, pred[256,4096]{1,0:T(8,128)(4,1)S(1)} %compare_and_fusion), kind=kOutput, calls=%fused_computation.8 | convolution fusion | flops 1107296256 | bytes 39329792 | tf_op jit(solution)/shard_map/cond/branch_1_fun/hqk,khd->qhd/dot_general | solution.py:153
  163.9 16.2 %fusion.2 = f32[8,256]{1,0:T(8,128)} fusion(f32[8,256,4096]{2,1,0:T(8,128)} %get-tuple-element.766, f32[8,256]{1,0:T(8,128)} %broadcast_maximum_fusion, pred[256,4096]{1,0:T(8,128)(4,1)S(1)} %compare_and_fusion), kind=kLoop, calls=%fused_computation.3 | loop fusion | flops 33552384 | bytes 34619392 | tf_op jit(solution)/shard_map/cond/branch_1_fun/reduce_sum | solution.py:152
  190.8 13.4 all-gather.19.cloned.1.call-done
  217.0 21.4 %all-gather.21.cloned.1.call-done = bf16[512,1024]{1,0:T(8,128)(2,1)} async-done(((bf16[256,1024]{1,0:T(8,128)(2,1)}), bf16[512,1024]{1,0:T(8,128)(2,1)}) %all-gather.21.cloned.1.call-update) | async-done | bytes 1048592 | tf_op jit(solution)/shard_map/all_gather | solution.py:51
  243.6 3.7 fusion.86
  247.3 7.0 add_convert_fusion
  267.7 6.1 fusion.85
  273.8 5.1 all-gather.25.cloned.1.call-done
  284.6 17.7 %all-gather.23.cloned.1.call-done = bf16[512,1024]{1,0:T(8,128)(2,1)} async-done(((bf16[256,1024]{1,0:T(8,128)(2,1)}), bf16[512,1024]{1,0:T(8,128)(2,1)}) %all-gather.23.cloned.1.call-update) | async-done | bytes 1048592 | tf_op jit(solution)/shard_map/all_gather | solution.py:51
  316.3 4.7 fusion.105
  325.8 11.7 all-gather.27.cloned.1.call-done
  344.6 374.5 %while.26 = (s32[]{:T(128)}, bf16[256,512]{0,1:T(8,128)(2,1)S(1)}, bf16[256,512]{0,1:T(8,128)(2,1)S(1)}, f32[256,512]{0,1:T(8,128)S(1)}, f32[256,512]{0,1:T(8,12...) while((s32[]{:T(128)}, bf16[256,512]{0,1:T(8,128)(2,1)S(1)}, ...), condition=%wide.region_29.30_spmd.clone, body=%wide.region_26.29_spmd.clone.sunk | while | flops 341115168 | bytes 29326032 | solution.py:294
  349.3 4.1 conditional.5
  372.4 4.4 collective-permute-start.2
  381.2 4.4 collective-permute-start.1
  396.7 6.5 collective-permute-start.3
  405.3 5.2 collective-permute-start.1
  423.2 7.0 collective-permute-start
  430.3 5.2 collective-permute-start.1
  451.1 9.3 collective-permute-start.1
  476.1 5.2 collective-permute-start.1
  497.0 5.2 collective-permute-start.1
  512.2 4.4 collective-permute-start.3
  516.6 4.9 collective-permute-start
  521.6 5.2 collective-permute-start.1
  539.2 7.3 collective-permute-start
  546.5 5.2 collective-permute-start.1
  567.4 7.5 collective-permute-start.1
  582.5 4.2 collective-permute-start.2
  592.4 5.2 collective-permute-start.1
  613.2 5.2 collective-permute-start.1
  631.1 6.7 collective-permute-start
  637.9 5.2 collective-permute-start.1
  655.5 7.3 collective-permute-start
  662.8 5.2 collective-permute-start.1
  683.7 5.8 collective-permute-start.1
  708.6 5.2 collective-permute-start.1
  730.5 25.3 %all-gather.29.cloned.1.call-done = bf16[512,1024]{1,0:T(8,128)(2,1)} async-done(((bf16[256,1024]{1,0:T(8,128)(2,1)}), bf16[512,1024]{1,0:T(8,128)(2,1)}) %all-gather.29.cloned.1.call-update) | async-done | bytes 1048592 | tf_op jit(solution)/shard_map/all_gather | solution.py:51
  759.0 68.1 %all-reduce.9 = (bf16[128,512]{0,1:T(8,128)(2,1)S(1)}, bf16[128,512]{0,1:T(8,128)(2,1)}, f32[1024]{0:T(1024)}, f32[1024]{0:T(1024)}, f32[1024]{0:T(1024)}, /*ind...) all-reduce(f32[128,512]{0,1:T(8,128)S(1)} %bitcast.154, ...), channel_id=1, replica_groups=mesh['blk'=16,'tp'=2] {'blk'}, use_global_device_ids=true, to_apply=%region_33.34 | all-reduce | flops 137216 | bytes 835584 | tf_op jit(solution)/shard_map/psum | solution.py:228
  844.4 6.3 all-reduce.6.cloned.1.call-done
  852.5 515.6 %all-reduce.8.cloned.1.call-done = (f32[1024,512]{1,0:T(8,128)}, f32[1024,512]{1,0:T(8,128)}, f32[1024,512]{1,0:T(8,128)}, f32[512,1024]{1,0:T(8,128)}, f32[1024...) async-done(((f32[1024,512]{1,0:T(8,128)}, f32[1024,512]{1,0:T(8,128)}, f32[1024,512]{1,0:T(8,128)}, f32[512,1024]{1,0:T(8,128)}, ...) | async-done | bytes 29360144 | tf_op jit(solution)/shard_map/psum | solution.py:328
  1381.6 4.3 copy.158
  (606 shorter events, 355.8 us)
Async XLA Ops:
  7.3 58.8 %all-gather.15.cloned.1.call-start = ((), (), s32[]{:S(2)}) async-start(), calls=%async_computation | async-start | bytes 4456448 | tf_op jit(solution)/shard_map/all_gather | solution.py:136
  12.7 105.2 %all-gather.17.cloned.1.call-start = ((), (), s32[]{:S(2)}) async-start(), calls=%async_computation.1 | async-start | bytes 4456448 | tf_op jit(solution)/shard_map/all_gather | solution.py:137
  14.0 190.2 %all-gather.19.cloned.1.call-start = ((), (), s32[]{:S(2)}) async-start(), calls=%async_computation.3 | async-start | bytes 1572864 | tf_op jit(solution)/shard_map/all_gather | solution.py:51
  184.2 54.2 %all-gather.21.cloned.1.call-start = ((), (), s32[]{:S(2)}) async-start(), calls=%async_computation.4 | async-start | bytes 1572864 | tf_op jit(solution)/shard_map/all_gather | solution.py:51
  217.0 61.9 %all-gather.25.cloned.1.call-start = ((), (), s32[]{:S(2)}) async-start(), calls=%async_computation.6 | async-start | bytes 1572864 | tf_op jit(solution)/shard_map/all_gather | solution.py:51
  257.5 44.8 %all-gather.23.cloned.1.call-start = ((), (), s32[]{:S(2)}) async-start(), calls=%async_computation.5 | async-start | bytes 1572864 | tf_op jit(solution)/shard_map/all_gather | solution.py:51
  263.3 74.1 %all-gather.27.cloned.1.call-start = ((), (), s32[]{:S(2)}) async-start(), calls=%async_computation.7 | async-start | bytes 1572864 | tf_op jit(solution)/shard_map/all_gather | solution.py:51
  316.0 439.8 %all-gather.29.cloned.1.call-start = ((), (), s32[]{:S(2)}) async-start(), calls=%async_computation.8 | async-start | bytes 1572864 | tf_op jit(solution)/shard_map/all_gather | solution.py:51
  353.5 11.4 collective-permute-start.3
  355.2 11.5 collective-permute-start
  372.4 13.2 collective-permute-start.2
  393.1 17.4 %collective-permute-start.2 = (bf16[256,512]{0,1:T(8,128)(2,1)S(1)}, bf16[256,512]{0,1:T(8,128)(2,1)S(1)}, u32[]{:S(2)}, u32[]{:S(2)}) collective-permute-start(bf16[256,512]{0,1:T(8,128)(2,1)S(1)} %convert_element_type.512), channel_id=1, source_target_pairs={{0,2},{2,4},{4,6},{6,8},{8,10},{10,12},{12,14},{14,16},{16,18},{18... | collective-permute-start | bytes 786440 | tf_op jit(solution)/shard_map/while/body/eval_jaxpr/ppermute | solution.py:19
  396.7 13.8 collective-permute-start.3
  418.0 17.4 %collective-permute-start.2 = (bf16[256,512]{0,1:T(8,128)(2,1)S(1)}, bf16[256,512]{0,1:T(8,128)(2,1)S(1)}, u32[]{:S(2)}, u32[]{:S(2)}) collective-permute-start(bf16[256,512]{0,1:T(8,128)(2,1)S(1)} %convert_element_type.512), channel_id=1, source_target_pairs={{0,2},{2,4},{4,6},{6,8},{8,10},{10,12},{12,14},{14,16},{16,18},{18... | collective-permute-start | bytes 786440 | tf_op jit(solution)/shard_map/while/body/eval_jaxpr/ppermute | solution.py:19
  420.8 14.7 %collective-permute-start.3 = (bf16[256,512]{0,1:T(8,128)(2,1)S(1)}, bf16[256,512]{0,1:T(8,128)(2,1)}, u32[]{:S(2)}, u32[]{:S(2)}) collective-permute-start(bf16[256,512]{0,1:T(8,128)(2,1)S(1)} %convert_element_type.514), channel_id=1, source_target_pairs={{0,2},{2,4},{4,6},{6,8},{8,10},{10,12},{12,14},{14,16},{16,18},{18... | collective-permute-start | bytes 786440 | tf_op jit(solution)/shard_map/while/body/eval_jaxpr/ppermute | solution.py:19
  423.2 14.1 %collective-permute-start = (bf16[256,512]{0,1:T(8,128)(2,1)S(1)}, bf16[256,512]{0,1:T(8,128)(2,1)S(1)}, u32[]{:S(2)}, u32[]{:S(2)}) collective-permute-start(bf16[256,512]{0,1:T(8,128)(2,1)S(1)} %copy.122), channel_id=1, source_target_pairs={{0,2},{2,4},{4,6},{6,8},{8,10},{10,12},{12,14},{14,16},{16,18},{18... | collective-permute-start | bytes 786440 | tf_op jit(solution)/shard_map/while/body/eval_jaxpr/ppermute | solution.py:14
  443.0 17.4 %collective-permute-start.2 = (bf16[256,512]{0,1:T(8,128)(2,1)S(1)}, bf16[256,512]{0,1:T(8,128)(2,1)S(1)}, u32[]{:S(2)}, u32[]{:S(2)}) collective-permute-start(bf16[256,512]{0,1:T(8,128)(2,1)S(1)} %convert_element_type.512), channel_id=1, source_target_pairs={{0,2},{2,4},{4,6},{6,8},{8,10},{10,12},{12,14},{14,16},{16,18},{18... | collective-permute-start | bytes 786440 | tf_op jit(solution)/shard_map/while/body/eval_jaxpr/ppermute | solution.py:19
  445.5 15.0 %collective-permute-start.3 = (bf16[256,512]{0,1:T(8,128)(2,1)S(1)}, bf16[256,512]{0,1:T(8,128)(2,1)}, u32[]{:S(2)}, u32[]{:S(2)}) collective-permute-start(bf16[256,512]{0,1:T(8,128)(2,1)S(1)} %convert_element_type.514), channel_id=1, source_target_pairs={{0,2},{2,4},{4,6},{6,8},{8,10},{10,12},{12,14},{14,16},{16,18},{18... | collective-permute-start | bytes 786440 | tf_op jit(solution)/shard_map/while/body/eval_jaxpr/ppermute | solution.py:19
  447.9 14.3 %collective-permute-start = (bf16[256,512]{0,1:T(8,128)(2,1)S(1)}, bf16[256,512]{0,1:T(8,128)(2,1)S(1)}, u32[]{:S(2)}, u32[]{:S(2)}) collective-permute-start(bf16[256,512]{0,1:T(8,128)(2,1)S(1)} %copy.122), channel_id=1, source_target_pairs={{0,2},{2,4},{4,6},{6,8},{8,10},{10,12},{12,14},{14,16},{16,18},{18... | collective-permute-start | bytes 786440 | tf_op jit(solution)/shard_map/while/body/eval_jaxpr/ppermute | solution.py:14
  468.0 13.3 collective-permute-start.2
  488.8 13.3 collective-permute-start.2
  509.7 17.1 %collective-permute-start.2 = (bf16[256,512]{0,1:T(8,128)(2,1)S(1)}, bf16[256,512]{0,1:T(8,128)(2,1)S(1)}, u32[]{:S(2)}, u32[]{:S(2)}) collective-permute-start(bf16[256,512]{0,1:T(8,128)(2,1)S(1)} %convert_element_type.512), channel_id=1, source_target_pairs={{0,2},{2,4},{4,6},{6,8},{8,10},{10,12},{12,14},{14,16},{16,18},{18... | collective-permute-start | bytes 786440 | tf_op jit(solution)/shard_map/while/body/eval_jaxpr/ppermute | solution.py:19
  512.2 14.6 %collective-permute-start.3 = (bf16[256,512]{0,1:T(8,128)(2,1)S(1)}, bf16[256,512]{0,1:T(8,128)(2,1)}, u32[]{:S(2)}, u32[]{:S(2)}) collective-permute-start(bf16[256,512]{0,1:T(8,128)(2,1)S(1)} %convert_element_type.514), channel_id=1, source_target_pairs={{0,2},{2,4},{4,6},{6,8},{8,10},{10,12},{12,14},{14,16},{16,18},{18... | collective-permute-start | bytes 786440 | tf_op jit(solution)/shard_map/while/body/eval_jaxpr/ppermute | solution.py:19
  516.6 12.0 collective-permute-start
  534.3 17.4 %collective-permute-start.2 = (bf16[256,512]{0,1:T(8,128)(2,1)S(1)}, bf16[256,512]{0,1:T(8,128)(2,1)S(1)}, u32[]{:S(2)}, u32[]{:S(2)}) collective-permute-start(bf16[256,512]{0,1:T(8,128)(2,1)S(1)} %convert_element_type.512), channel_id=1, source_target_pairs={{0,2},{2,4},{4,6},{6,8},{8,10},{10,12},{12,14},{14,16},{16,18},{18... | collective-permute-start | bytes 786440 | tf_op jit(solution)/shard_map/while/body/eval_jaxpr/ppermute | solution.py:19
  536.8 15.0 %collective-permute-start.3 = (bf16[256,512]{0,1:T(8,128)(2,1)S(1)}, bf16[256,512]{0,1:T(8,128)(2,1)}, u32[]{:S(2)}, u32[]{:S(2)}) collective-permute-start(bf16[256,512]{0,1:T(8,128)(2,1)S(1)} %convert_element_type.514), channel_id=1, source_target_pairs={{0,2},{2,4},{4,6},{6,8},{8,10},{10,12},{12,14},{14,16},{16,18},{18... | collective-permute-start | bytes 786440 | tf_op jit(solution)/shard_map/while/body/eval_jaxpr/ppermute | solution.py:19
  539.2 14.3 %collective-permute-start = (bf16[256,512]{0,1:T(8,128)(2,1)S(1)}, bf16[256,512]{0,1:T(8,128)(2,1)S(1)}, u32[]{:S(2)}, u32[]{:S(2)}) collective-permute-start(bf16[256,512]{0,1:T(8,128)(2,1)S(1)} %copy.122), channel_id=1, source_target_pairs={{0,2},{2,4},{4,6},{6,8},{8,10},{10,12},{12,14},{14,16},{16,18},{18... | collective-permute-start | bytes 786440 | tf_op jit(solution)/shard_map/while/body/eval_jaxpr/ppermute | solution.py:14
  559.3 15.7 %collective-permute-start.2 = (bf16[256,512]{0,1:T(8,128)(2,1)S(1)}, bf16[256,512]{0,1:T(8,128)(2,1)S(1)}, u32[]{:S(2)}, u32[]{:S(2)}) collective-permute-start(bf16[256,512]{0,1:T(8,128)(2,1)S(1)} %convert_element_type.512), channel_id=1, source_target_pairs={{0,2},{2,4},{4,6},{6,8},{8,10},{10,12},{12,14},{14,16},{16,18},{18... | collective-permute-start | bytes 786440 | tf_op jit(solution)/shard_map/while/body/eval_jaxpr/ppermute | solution.py:19
  561.8 13.2 collective-permute-start.3
  564.2 12.6 collective-permute-start
  582.5 15.1 %collective-permute-start.2 = (bf16[256,512]{0,1:T(8,128)(2,1)S(1)}, bf16[256,512]{0,1:T(8,128)(2,1)S(1)}, u32[]{:S(2)}, u32[]{:S(2)}) collective-permute-start(bf16[256,512]{0,1:T(8,128)(2,1)S(1)} %convert_element_type.512), channel_id=1, source_target_pairs={{0,2},{2,4},{4,6},{6,8},{8,10},{10,12},{12,14},{14,16},{16,18},{18... | collective-permute-start | bytes 786440 | tf_op jit(solution)/shard_map/while/body/eval_jaxpr/ppermute | solution.py:19
  605.1 13.3 collective-permute-start.2
  607.6 12.9 collective-permute-start.3
  610.0 12.3 collective-permute-start
  628.0 15.1 %collective-permute-start.2 = (bf16[256,512]{0,1:T(8,128)(2,1)S(1)}, bf16[256,512]{0,1:T(8,128)(2,1)S(1)}, u32[]{:S(2)}, u32[]{:S(2)}) collective-permute-start(bf16[256,512]{0,1:T(8,128)(2,1)S(1)} %convert_element_type.512), channel_id=1, source_target_pairs={{0,2},{2,4},{4,6},{6,8},{8,10},{10,12},{12,14},{14,16},{16,18},{18... | collective-permute-start | bytes 786440 | tf_op jit(solution)/shard_map/while/body/eval_jaxpr/ppermute | solution.py:19
  628.5 16.1 %collective-permute-start.3 = (bf16[256,512]{0,1:T(8,128)(2,1)S(1)}, bf16[256,512]{0,1:T(8,128)(2,1)}, u32[]{:S(2)}, u32[]{:S(2)}) collective-permute-start(bf16[256,512]{0,1:T(8,128)(2,1)S(1)} %convert_element_type.514), channel_id=1, source_target_pairs={{0,2},{2,4},{4,6},{6,8},{8,10},{10,12},{12,14},{14,16},{16,18},{18... | collective-permute-start | bytes 786440 | tf_op jit(solution)/shard_map/while/body/eval_jaxpr/ppermute | solution.py:19
  631.1 15.2 %collective-permute-start = (bf16[256,512]{0,1:T(8,128)(2,1)S(1)}, bf16[256,512]{0,1:T(8,128)(2,1)S(1)}, u32[]{:S(2)}, u32[]{:S(2)}) collective-permute-start(bf16[256,512]{0,1:T(8,128)(2,1)S(1)} %copy.122), channel_id=1, source_target_pairs={{0,2},{2,4},{4,6},{6,8},{8,10},{10,12},{12,14},{14,16},{16,18},{18... | collective-permute-start | bytes 786440 | tf_op jit(solution)/shard_map/while/body/eval_jaxpr/ppermute | solution.py:14
  652.1 15.9 %collective-permute-start.2 = (bf16[256,512]{0,1:T(8,128)(2,1)S(1)}, bf16[256,512]{0,1:T(8,128)(2,1)S(1)}, u32[]{:S(2)}, u32[]{:S(2)}) collective-permute-start(bf16[256,512]{0,1:T(8,128)(2,1)S(1)} %convert_element_type.512), channel_id=1, source_target_pairs={{0,2},{2,4},{4,6},{6,8},{8,10},{10,12},{12,14},{14,16},{16,18},{18... | collective-permute-start | bytes 786440 | tf_op jit(solution)/shard_map/while/body/eval_jaxpr/ppermute | solution.py:19
  653.1 15.6 %collective-permute-start.3 = (bf16[256,512]{0,1:T(8,128)(2,1)S(1)}, bf16[256,512]{0,1:T(8,128)(2,1)}, u32[]{:S(2)}, u32[]{:S(2)}) collective-permute-start(bf16[256,512]{0,1:T(8,128)(2,1)S(1)} %convert_element_type.514), channel_id=1, source_target_pairs={{0,2},{2,4},{4,6},{6,8},{8,10},{10,12},{12,14},{14,16},{16,18},{18... | collective-permute-start | bytes 786440 | tf_op jit(solution)/shard_map/while/body/eval_jaxpr/ppermute | solution.py:19
  655.5 14.9 %collective-permute-start = (bf16[256,512]{0,1:T(8,128)(2,1)S(1)}, bf16[256,512]{0,1:T(8,128)(2,1)S(1)}, u32[]{:S(2)}, u32[]{:S(2)}) collective-permute-start(bf16[256,512]{0,1:T(8,128)(2,1)S(1)} %copy.122), channel_id=1, source_target_pairs={{0,2},{2,4},{4,6},{6,8},{8,10},{10,12},{12,14},{14,16},{16,18},{18... | collective-permute-start | bytes 786440 | tf_op jit(solution)/shard_map/while/body/eval_jaxpr/ppermute | solution.py:14
  676.1 13.7 collective-permute-start.2
  678.0 14.7 %collective-permute-start.3 = (bf16[256,512]{0,1:T(8,128)(2,1)S(1)}, bf16[256,512]{0,1:T(8,128)(2,1)}, u32[]{:S(2)}, u32[]{:S(2)}) collective-permute-start(bf16[256,512]{0,1:T(8,128)(2,1)S(1)} %convert_element_type.514), channel_id=1, source_target_pairs={{0,2},{2,4},{4,6},{6,8},{8,10},{10,12},{12,14},{14,16},{16,18},{18... | collective-permute-start | bytes 786440 | tf_op jit(solution)/shard_map/while/body/eval_jaxpr/ppermute | solution.py:19
  680.5 14.0 %collective-permute-start = (bf16[256,512]{0,1:T(8,128)(2,1)S(1)}, bf16[256,512]{0,1:T(8,128)(2,1)S(1)}, u32[]{:S(2)}, u32[]{:S(2)}) collective-permute-start(bf16[256,512]{0,1:T(8,128)(2,1)S(1)} %copy.122), channel_id=1, source_target_pairs={{0,2},{2,4},{4,6},{6,8},{8,10},{10,12},{12,14},{14,16},{16,18},{18... | collective-permute-start | bytes 786440 | tf_op jit(solution)/shard_map/while/body/eval_jaxpr/ppermute | solution.py:14
  700.2 14.3 %collective-permute-start.2 = (bf16[256,512]{0,1:T(8,128)(2,1)S(1)}, bf16[256,512]{0,1:T(8,128)(2,1)S(1)}, u32[]{:S(2)}, u32[]{:S(2)}) collective-permute-start(bf16[256,512]{0,1:T(8,128)(2,1)S(1)} %convert_element_type.512), channel_id=1, source_target_pairs={{0,2},{2,4},{4,6},{6,8},{8,10},{10,12},{12,14},{14,16},{16,18},{18... | collective-permute-start | bytes 786440 | tf_op jit(solution)/shard_map/while/body/eval_jaxpr/ppermute | solution.py:19
  703.0 14.4 %collective-permute-start.3 = (bf16[256,512]{0,1:T(8,128)(2,1)S(1)}, bf16[256,512]{0,1:T(8,128)(2,1)}, u32[]{:S(2)}, u32[]{:S(2)}) collective-permute-start(bf16[256,512]{0,1:T(8,128)(2,1)S(1)} %convert_element_type.514), channel_id=1, source_target_pairs={{0,2},{2,4},{4,6},{6,8},{8,10},{10,12},{12,14},{14,16},{16,18},{18... | collective-permute-start | bytes 786440 | tf_op jit(solution)/shard_map/while/body/eval_jaxpr/ppermute | solution.py:19
  705.4 13.7 collective-permute-start
  723.7 127.0 %all-reduce.6.cloned.1.call-start = ((), (), s32[]{:S(2)}) async-start(), calls=%async_computation.2 | async-start | bytes 524288 | tf_op jit(solution)/shard_map/psum | solution.py:239
  831.0 537.1 %all-reduce.8.cloned.1.call-start = ((), (), s32[]{:S(2)}) async-start(), calls=%async_computation.9 | async-start | bytes 58720256 | tf_op jit(solution)/shard_map/psum | solution.py:328
  (122 other events, 968.3 us)
Sparse Core Ops, SparseCore 0:
  12.8 53.2 all-gather.14
  68.8 49.0 all-gather.16
  184.3 19.7 all-gather.18
  217.1 21.2 all-gather.20
  257.6 21.2 all-gather.24
  280.9 21.2 all-gather.22
  316.1 21.2 all-gather.26
  723.8 31.9 all-gather.28
  831.1 19.5 all-reduce.5
  858.5 509.4 all-reduce.7
